TPU v7x, 32 devices: a whole 2x2x4 slice. The times are simulated.
32 devices in a mesh: tile: 8 (over z, core), grp: 4 (over y, x).
Axes of the slice: x: 2, y: 2, z: 4, core: 2. Of those that a mesh axis runs over, the one named last changes fastest.
Arguments:
- spectra: bfloat16 [128, 16, 1024], P(('tile', 'grp')), may hold values from -320 to 320
- validity: int32 [128, 16], P(('tile', 'grp')), may hold values 0 or 1
- source_lists: int32 [8, 4, 16], P(None, 'grp'), may hold values from 0 to 127, as said below
Outputs:
- correlations: bfloat16 [8, 4, 16, 16, 2048], P('tile', 'grp')
Inputs may be any that keep to these rules, and one draw needn't show every extreme that they name: `source_lists`: entry [t, g, j] names a channel held by a device of grp index g, that is (entry // 4) % 4 == g; the 16 entries of one list are distinct; at most 2 entries of one list are held by any one device, and in every list some device holds exactly 2.
All inputs are finite; a program needn't handle non-finite values. No bound on the sum of `validity` on one device may be relied on, other than what follows from the above.
Results may differ from a plain program's by a relative error of at most 0.0066.
Values may be sent and summed in bfloat16 or wider, within the bound.
No kernel may reach another device: no remote copies, remote signals or barrier semaphores. Data moves between devices by JAX's collectives and lax.ppermute only.
A program may use at most 128 MiB of HBM per device.

v0:
```python
import math
import jax
import jax.numpy as jnp
from jax import lax
from jax.sharding import PartitionSpec as P

LAGS = 2048
SMOOTH = 64
EPSILON = 1e-06


def box_mean(magnitude, reach):
    bin_count = magnitude.shape[-1]
    lead_shape = magnitude.shape[:-1]
    running = jnp.cumsum(magnitude, axis=-1)
    prefix = jnp.concatenate([jnp.zeros(lead_shape + (1,), magnitude.dtype), running], axis=-1)
    tail = jnp.broadcast_to(prefix[..., -1:], lead_shape + (reach,))
    upper = jnp.concatenate([prefix[..., reach + 1 :], tail], axis=-1)
    lower = jnp.concatenate(
        [jnp.zeros(lead_shape + (reach,), magnitude.dtype), prefix[..., : bin_count - reach]],
        axis=-1,
    )
    bin_index = jnp.arange(bin_count, dtype=jnp.int32)
    counted = jnp.minimum(bin_index + reach + 1, bin_count) - jnp.maximum(bin_index - reach, 0)
    return (upper - lower) / counted.astype(magnitude.dtype)


def whiten(spectra, reach):
    bin_count = spectra.shape[-1] // 2
    real_part = spectra[..., :bin_count].astype(jnp.float32)
    imag_part = spectra[..., bin_count:].astype(jnp.float32)
    magnitude = jnp.sqrt(real_part * real_part + imag_part * imag_part)
    smoothed = box_mean(magnitude, reach)
    inverse = 1.0 / (smoothed + EPSILON)
    return jnp.concatenate([real_part * inverse, imag_part * inverse], axis=-1).astype(jnp.bfloat16)


def lag_table(bin_count, lag_count):
    frequency = jnp.arange(bin_count, dtype=jnp.int32)[:, None]
    lag_shift = jnp.arange(lag_count, dtype=jnp.int32)[None, :] - lag_count // 2
    phase_index = frequency * lag_shift % (2 * lag_count)
    angles = phase_index.astype(jnp.float32) * (math.pi / lag_count)
    return jnp.concatenate([jnp.cos(angles), -jnp.sin(angles)], axis=0).astype(jnp.bfloat16)


def correlate(source_rows, source_mask, panel_rows, panel_mask, lag_basis):
    bin_count = source_rows.shape[-1] // 2
    masked_source = source_rows * source_mask[:, :, None]
    masked_panel = panel_rows * panel_mask[:, :, None]
    source_real = masked_source[..., :bin_count]
    source_imag = masked_source[..., bin_count:]
    panel_real = masked_panel[..., :bin_count]
    panel_imag = masked_panel[..., bin_count:]
    real_sum = jnp.einsum(
        "swf,rwf->srf", source_real, panel_real, preferred_element_type=jnp.float32
    ) + jnp.einsum("swf,rwf->srf", source_imag, panel_imag, preferred_element_type=jnp.float32)
    imag_sum = jnp.einsum(
        "swf,rwf->srf", source_real, panel_imag, preferred_element_type=jnp.float32
    ) - jnp.einsum("swf,rwf->srf", source_imag, panel_real, preferred_element_type=jnp.float32)
    shared_count = jnp.dot(source_mask, panel_mask.T, preferred_element_type=jnp.float32)
    weight = (1.0 / jnp.maximum(shared_count, 1.0))[:, :, None]
    stacked = jnp.concatenate([real_sum * weight, imag_sum * weight], axis=-1).astype(jnp.bfloat16)
    lagged = jnp.dot(
        stacked.reshape(-1, 2 * bin_count), lag_basis, preferred_element_type=jnp.float32
    )
    lagged = lagged * (1.0 / math.sqrt(bin_count))
    return lagged.reshape(source_rows.shape[0], panel_rows.shape[0], -1).astype(jnp.bfloat16)


def body(spectra, validity, source_lists):
    group_count = lax.axis_size("grp")
    ch_local = spectra.shape[0]
    row_width = spectra.shape[2]
    tile_here = lax.axis_index("tile")
    all_lists = source_lists[:, 0, :]
    block_span = ch_local * group_count
    own_list = lax.dynamic_index_in_dim(all_lists, tile_here, 0, keepdims=False)
    owner_tile = own_list // block_span
    local_row = own_list % ch_local
    mask_rows = validity.astype(jnp.bfloat16)
    ready = whiten(spectra, SMOOTH)
    column_rows, column_mask = (
        lax.all_gather(ready, "tile", axis=0, tiled=True),
        lax.all_gather(mask_rows, "tile", axis=0, tiled=True),
    )
    picked = owner_tile * ch_local + local_row
    source_rows = jnp.take(column_rows, picked, axis=0)
    source_mask = jnp.take(column_mask, picked, axis=0)
    panel_rows, panel_mask = (
        lax.all_gather(ready, "grp", axis=0, tiled=True),
        lax.all_gather(mask_rows, "grp", axis=0, tiled=True),
    )
    lag_basis = lag_table(row_width // 2, LAGS)
    lagged = correlate(source_rows, source_mask, panel_rows, panel_mask, lag_basis)
    return lagged[None, None]


def solution(mesh):
    in_specs = (P(("tile", "grp"), None, None), P(("tile", "grp"), None), P(None, "grp", None))
    out_specs = P("tile", "grp", None, None, None)
    return jax.shard_map(body, mesh=mesh, in_specs=in_specs, out_specs=out_specs, check_vma=False)
```

profile of v0, /device:TPU:0, one launch (start us, length us, event | category | flops | bytes accessed | tf_op | source)
XLA Modules:
  0.0 140.3 jit_solution(8925865290935990632)
XLA Ops:
  7.5 4.6 %reduce-window.6 = f32[4,16,4,128]{3,1,2,0:T(8,128)S(1)} reduce-window(f32[4,16,4,128]{3,1,2,0:T(8,128)S(1)} %copy_bitcast_fusion.1, f32[]{:T(128)} %constant.90.clone.1), window={size=1x1x1x128 pad=0_0x0_0x0_0x127_0}, to_apply=%region_0.1 | reduce-window | flops 4161536 | bytes 262148 | tf_op jit(solution)/shard_map/reduce-window
  12.8 1.0 fusion.37
  16.6 11.9 %all_gather.12 = bf16[16,16,1024]{2,1,0:T(8,128)(2,1)S(1)} all-gather(bf16[4,16,1024]{2,1,0:T(8,128)(2,1)} %pad_maximum_fusion), channel_id=1, replica_groups=mesh['tile'=8,'grp'=4] {'grp'}, dimensions={0}, use_global_device_ids=true | all-gather | bytes 655360 | tf_op jit(solution)/shard_map/all_gather | solution.py:90
  29.2 12.0 %all-gather.1 = bf16[8,4,16]{2,1,0:T(4,128)(2,1)S(1)} all-gather(bf16[1,4,16]{2,1,0:T(4,128)(2,1)S(1)} %convert_bitcast_fusion), channel_id=1, replica_groups=mesh['tile'=8,'grp'=4] {'tile'}, dimensions={0}, use_global_device_ids=true | all-gather | bytes 1152 | tf_op jit(solution)/shard_map/all_gather | solution.py:84
  41.2 7.7 %all-gather = bf16[4,4,16]{2,1,0:T(4,128)(2,1)S(1)} all-gather(bf16[1,4,16]{2,1,0:T(4,128)(2,1)S(1)} %convert_bitcast_fusion), channel_id=1, replica_groups=mesh['tile'=8,'grp'=4] {'grp'}, dimensions={0}, use_global_device_ids=true | all-gather | bytes 640 | tf_op jit(solution)/shard_map/all_gather | solution.py:91
  48.9 4.7 %copy.39 = bf16[16,16,1024]{1,0,2:T(8,128)(2,1)} copy(bf16[16,16,1024]{2,1,0:T(8,128)(2,1)S(1)} %all_gather.12) | data formatting | bytes 1048576 | tf_op jit(solution)/shard_map/all_gather | solution.py:90
  53.6 4.5 %fusion.66 = bf16[16,16,1024]{1,0,2:T(8,128)(2,1)} fusion(bf16[16,16,1024]{1,0,2:T(8,128)(2,1)} %copy.39, bf16[16,16]{1,0:T(8,128)(2,1)S(1)} %bitcast.68), kind=kLoop, calls=%fused_computation.18.clone.1 | loop fusion | flops 262144 | bytes 1049088 | tf_op jit(solution)/shard_map/swf,rwf->srf/dot_general | solution.py:56
  58.2 2.2 %fusion.70 = bf16[16,16,1024]{1,0,2:T(8,128)(2,1)} fusion(bf16[16,16,1024]{1,0,2:T(8,128)(2,1)S(1)} %copy-done, bf16[16,16]{1,0:T(8,128)(2,1)S(1)} %bitcast.69), kind=kLoop, calls=%fused_computation.22.clone | loop fusion | flops 262144 | bytes 1049088 | tf_op jit(solution)/shard_map/swf,rwf->srf/dot_general | solution.py:57
  61.8 4.6 %fusion.72 = bf16[16,16,1024]{1,0,2:T(8,128)(2,1)} fusion(bf16[16,16,1024]{1,0,2:T(8,128)(2,1)} %copy.39, bf16[16,16]{1,0:T(8,128)(2,1)S(1)} %bitcast.71), kind=kLoop, calls=%fused_computation.24.clone | loop fusion | flops 262144 | bytes 1049088 | tf_op jit(solution)/shard_map/swf,rwf->srf/dot_general | solution.py:59
  66.4 2.2 %fusion.68 = bf16[16,16,1024]{1,0,2:T(8,128)(2,1)} fusion(bf16[16,16,1024]{1,0,2:T(8,128)(2,1)S(1)} %copy-done.1, bf16[16,16]{1,0:T(8,128)(2,1)S(1)} %bitcast.72), kind=kLoop, calls=%fused_computation.20.clone.1 | loop fusion | flops 262144 | bytes 1049088 | tf_op jit(solution)/shard_map/swf,rwf->srf/dot_general | solution.py:54
  68.6 18.0 %cosine_convert_fusion = (bf16[512,2048]{1,0:T(8,128)(2,1)}, bf16[512,2048]{1,0:T(8,128)(2,1)}) fusion(s32[2048]{0:T(1024)S(1)} %iota_add_fusion), kind=kLoop, calls=%fused_computation.13 | loop fusion | flops 17825792 | bytes 4202496 | tf_op jit(solution)/shard_map/convert
  86.7 1.8 %gather_fusion = bf16[16,16,1024]{2,1,0:T(8,128)(2,1)S(1)} fusion(bf16[32,16,1024]{2,1,0:T(8,128)(2,1)} %all-gather.4.cloned.1.call-done, s32[1024]{0:T(1024)S(1)} %pad_clamp_fusion), kind=kCustom, calls=%fused_computation | custom fusion | bytes 1048640 | tf_op jit(solution)/shard_map/jit(_take)/gather | solution.py:87
  89.4 2.0 %copy.41 = bf16[16,16,512]{1,0,2:T(8,128)(2,1)S(1)} copy(bf16[16,16,512]{2,1,0:T(8,128)(2,1)S(1)} %get-tuple-element.7) | data formatting | bytes 524288 | tf_op jit(solution)/shard_map/slice | solution.py:51
  91.3 5.5 %fusion.10 = f32[512,16,16]{2,1,0:T(8,128)} fusion(bf16[16,16,512]{1,0,2:T(8,128)(2,1)S(1)} %copy.41, bf16[16,16,1024]{1,0,2:T(8,128)(2,1)} %fusion.66), kind=kOutput, calls=%fused_computation.17 | convolution fusion | flops 4194304 | bytes 1310720 | tf_op jit(solution)/shard_map/swf,rwf->srf/dot_general | solution.py:56
  96.8 3.6 %copy.43 = f32[512,16,16]{0,1,2:T(8,128)} copy(f32[512,16,16]{2,1,0:T(8,128)} %fusion.10) | data formatting | bytes 1048576 | tf_op jit(solution)/shard_map/swf,rwf->srf/dot_general | solution.py:56
  100.5 2.0 %copy.40 = bf16[16,16,512]{1,0,2:T(8,128)(2,1)S(1)} copy(bf16[16,16,512]{2,1,0:T(8,128)(2,1)S(1)} %copy-done.9) | data formatting | bytes 524288 | tf_op jit(solution)/shard_map/slice | solution.py:50
  102.5 1.3 copy-done.4
  103.8 4.7 %fusion.14 = f32[512,16,16]{2,1,0:T(8,128)} fusion(bf16[16,16,512]{1,0,2:T(8,128)(2,1)S(1)} %copy.40, bf16[16,16,1024]{1,0,2:T(8,128)(2,1)} %fusion.70), kind=kOutput, calls=%fused_computation.21 | convolution fusion | flops 4194304 | bytes 1310720 | tf_op jit(solution)/shard_map/swf,rwf->srf/dot_general | solution.py:57
  108.5 3.8 %copy.46 = f32[512,16,16]{0,1,2:T(8,128)} copy(f32[512,16,16]{2,1,0:T(8,128)} %fusion.14) | data formatting | bytes 1048576 | tf_op jit(solution)/shard_map/swf,rwf->srf/dot_general | solution.py:57
  112.3 4.8 %fusion.16 = f32[512,16,16]{2,1,0:T(8,128)} fusion(bf16[16,16,512]{1,0,2:T(8,128)(2,1)S(1)} %copy-done.3, bf16[16,16,1024]{1,0,2:T(8,128)(2,1)} %fusion.72), kind=kOutput, calls=%fused_computation.23 | convolution fusion | flops 4194304 | bytes 1310720 | tf_op jit(solution)/shard_map/swf,rwf->srf/dot_general | solution.py:59
  117.1 3.8 %copy.47 = f32[512,16,16]{0,1,2:T(8,128)} copy(f32[512,16,16]{2,1,0:T(8,128)} %fusion.16) | data formatting | bytes 1048576 | tf_op jit(solution)/shard_map/swf,rwf->srf/dot_general | solution.py:59
  120.9 4.8 %fusion.12 = f32[512,16,16]{2,1,0:T(8,128)} fusion(bf16[16,16,512]{1,0,2:T(8,128)(2,1)S(1)} %copy-done.5, bf16[16,16,1024]{1,0,2:T(8,128)(2,1)} %fusion.68), kind=kOutput, calls=%fused_computation.19 | convolution fusion | flops 4194304 | bytes 1310720 | tf_op jit(solution)/shard_map/swf,rwf->srf/dot_general | solution.py:54
  125.6 3.1 %copy.42 = f32[512,16,16]{0,1,2:T(8,128)S(1)} copy(f32[512,16,16]{2,1,0:T(8,128)} %fusion.12) | data formatting | bytes 1048576 | tf_op jit(solution)/shard_map/swf,rwf->srf/dot_general | solution.py:54
  129.0 4.5 %fusion.21 = bf16[256,2048]{1,0:T(8,128)(2,1)} fusion(bf16[512,2048]{1,0:T(8,128)(2,1)} %get-tuple-element.14, bf16[512,2048]{1,0:T(8,128)(2,1)} %get-tuple-element.13, bf16[256,512]{1,0:T(8,128)(2,1)S(1)} %bitcast.66, bf16[256,512]{1,0:T(8,128)(2,1)S(1)} %bitcast.65), kind=kOutput, calls=%fused_computation.26 | convolution fusion | flops 1084227584 | bytes 5767168 | tf_op jit(solution)/shard_map/dot_general | solution.py:63
  (46 shorter events, 7.7 us)
Async XLA Ops:
  6.5 80.1 %all-gather.4.cloned.1.call-start = ((), (), s32[]{:S(2)}) async-start(), calls=%async_computation | async-start | bytes 1179648 | tf_op jit(solution)/shard_map/all_gather | solution.py:83
  53.6 4.6 %copy-start = (bf16[16,16,1024]{1,0,2:T(8,128)(2,1)S(1)}, bf16[16,16,1024]{1,0,2:T(8,128)(2,1)}, u32[]{:S(2)}) copy-start(bf16[16,16,1024]{1,0,2:T(8,128)(2,1)} %copy.39) | copy-start | bytes 1572868
  61.8 4.6 %copy-start.1 = (bf16[16,16,1024]{1,0,2:T(8,128)(2,1)S(1)}, bf16[16,16,1024]{1,0,2:T(8,128)(2,1)}, u32[]{:S(2)}) copy-start(bf16[16,16,1024]{1,0,2:T(8,128)(2,1)} %copy.39) | copy-start | bytes 1572868
  91.3 5.5 %copy-start.2 = (bf16[16,16,512]{1,0,2:T(8,128)(2,1)}, bf16[16,16,512]{1,0,2:T(8,128)(2,1)S(1)}, u32[]{:S(2)}) copy-start(bf16[16,16,512]{1,0,2:T(8,128)(2,1)S(1)} %copy.41) | copy-start | bytes 786436
  96.8 3.6 %copy-start.9 = (bf16[16,16,512]{2,1,0:T(8,128)(2,1)S(1)}, bf16[16,16,512]{2,1,0:T(8,128)(2,1)}, u32[]{:S(2)}) copy-start(bf16[16,16,512]{2,1,0:T(8,128)(2,1)} %get-tuple-element.8) | copy-start | bytes 786436
  102.5 1.3 copy-start.4
  108.5 3.8 %copy-start.3 = (bf16[16,16,512]{1,0,2:T(8,128)(2,1)S(1)}, bf16[16,16,512]{1,0,2:T(8,128)(2,1)}, u32[]{:S(2)}) copy-start(bf16[16,16,512]{1,0,2:T(8,128)(2,1)} %copy-done.2) | copy-start | bytes 786436
  117.0 3.8 %copy-start.5 = (bf16[16,16,512]{1,0,2:T(8,128)(2,1)S(1)}, bf16[16,16,512]{1,0,2:T(8,128)(2,1)}, u32[]{:S(2)}) copy-start(bf16[16,16,512]{1,0,2:T(8,128)(2,1)} %copy-done.4) | copy-start | bytes 786436
  125.6 3.1 %copy-start.6 = (f32[512,16,16]{0,1,2:T(8,128)S(1)}, f32[512,16,16]{0,1,2:T(8,128)}, u32[]{:S(2)}) copy-start(f32[512,16,16]{0,1,2:T(8,128)} %copy.43) | copy-start | bytes 1572868
  125.6 3.1 %copy-start.7 = (f32[512,16,16]{0,1,2:T(8,128)S(1)}, f32[512,16,16]{0,1,2:T(8,128)}, u32[]{:S(2)}) copy-start(f32[512,16,16]{0,1,2:T(8,128)} %copy.46) | copy-start | bytes 1572868
  125.6 3.1 %copy-start.8 = (f32[512,16,16]{0,1,2:T(8,128)S(1)}, f32[512,16,16]{0,1,2:T(8,128)}, u32[]{:S(2)}) copy-start(f32[512,16,16]{0,1,2:T(8,128)} %copy.47) | copy-start | bytes 1572868
  125.6 3.1 %copy-start.10 = (f32[16,16]{1,0:T(8,128)S(1)}, f32[16,16]{1,0:T(8,128)}, u32[]{:S(2)}) copy-start(f32[16,16]{1,0:T(8,128)} %fusion.28) | copy-start | bytes 3076
Sparse Core Ops, SparseCore 0:
  15.4 24.9 all-gather.3
where the time goes:
time: 141 us; the launch traced here: 140 us
  other arithmetic  42.2 us (30%)
  blocking collectives  31.6 us (22%)
  local copies, waits for them, and re-layouts  28 us (20%)
  matrix products  25 us (18%)
  between operations  13.6 us (10%)
    another operation x7, other arithmetic  24.7 us
    all_gather x1, blocking collectives, body(): lax.all_gather(mask_rows, 'tile', axis=0, tiled=True)  12 us
    all_gather x1, blocking collectives, body(): lax.all_gather(ready, 'grp', axis=0, tiled=True)  11.9 us
    all_gather x1, blocking collectives, body(): lax.all_gather(mask_rows, 'grp', axis=0, tiled=True)  7.7 us
    dot_general x1, matrix products, correlate(): jnp.einsum('swf,rwf->srf', source_imag, panel_imag, preferred_element_typ...  5.49 us
    dot_general x1, matrix products, correlate(): jnp.einsum('swf,rwf->srf', source_real, panel_real, preferred_element_typ...  4.78 us
    dot_general x1, matrix products, correlate(): jnp.einsum('swf,rwf->srf', source_imag, panel_real, preferred_element_typ...  4.76 us
    dot_general x1, matrix products, correlate(): jnp.einsum('swf,rwf->srf', source_real, panel_imag, preferred_element_typ...  4.73 us
  transfers between devices with their start and end apart: 1, of which 0 were waited for; matrix products, arithmetic and copies ran while one was open for 28% of the time, Pallas kernels for 0%

commit v1 on v0

--- a/solution.py
+++ b/solution.py
@@ -7,6 +7,27 @@
 LAGS = 2048
 SMOOTH = 64
 EPSILON = 1e-06
+
+
+def gather_around(x, axis, dim):
+    peers, index, width = (lax.axis_size(axis), lax.axis_index(axis), x.shape[dim])
+    ahead = [(i, (i + 1) % peers) for i in range(peers)]
+    behind = [(i, (i - 1) % peers) for i in range(peers)]
+    out = jnp.zeros((*x.shape[:dim], peers * width, *x.shape[dim + 1 :]), x.dtype)
+    out = lax.dynamic_update_slice_in_dim(out, x, index * width, axis=dim)
+    from_left = from_right = x
+    halfway = peers // 2
+    for hop in range(1, halfway + 1):
+        from_left = lax.ppermute(from_left, axis, ahead)
+        out = lax.dynamic_update_slice_in_dim(
+            out, from_left, (index - hop) % peers * width, axis=dim
+        )
+        if hop < peers - halfway:
+            from_right = lax.ppermute(from_right, axis, behind)
+            out = lax.dynamic_update_slice_in_dim(
+                out, from_right, (index + hop) % peers * width, axis=dim
+            )
+    return out
 
 
 def box_mean(magnitude, reach):
@@ -87,7 +108,7 @@
     source_rows = jnp.take(column_rows, picked, axis=0)
     source_mask = jnp.take(column_mask, picked, axis=0)
     panel_rows, panel_mask = (
-        lax.all_gather(ready, "grp", axis=0, tiled=True),
+        gather_around(ready, "grp", 0),
         lax.all_gather(mask_rows, "grp", axis=0, tiled=True),
     )
     lag_basis = lag_table(row_width // 2, LAGS)

time: 141 us -> 148 us (1.050)
  blocking collectives: 31.6 us -> 20.5 us
  local copies, waits for them, and re-layouts: 28 us -> 35 us
  starting transfers between devices: 0.01 us -> 4.72 us
  other arithmetic: 42.2 us -> 45.7 us
  waiting for transfers between devices: 0.02 us -> 2.5 us
    all_gather x1 -> x0, blocking collectives: 11.9 us -> none  [body(): lax.all_gather(ready, 'grp', axis=0, tiled=True)]
    dynamic_update_slice x0 -> x4, local copies, waits for them, and re-layouts: none -> 5.63 us  [the longest x2 2.87 us: gather_around(): lax.dynamic_update_slice_in_dim(out, from_left, (index - hop) % peers * w...]
    all_gather x1 -> x0, local copies, waits for them, and re-layouts: 4.72 us -> none  [body(): lax.all_gather(ready, 'grp', axis=0, tiled=True)]
    ppermute x0 -> x3, starting transfers between devices: none -> 4.72 us  [the longest x2 3.69 us: gather_around(): from_left = lax.ppermute(from_left, axis, ahead)]
    broadcast_in_dim x0 -> x1, local copies, waits for them, and re-layouts: none -> 2.48 us  [gather_around(): jnp.zeros((*x.shape[:dim], peers * width, *x.shape[dim + 1:]), x.dtype)]
    ppermute x0 -> x3, waiting for transfers between devices: none -> 2.48 us  [the longest x2 2.48 us: gather_around(): from_left = lax.ppermute(from_left, axis, ahead)]
    dot_general x1, other arithmetic: 2.24 us -> 4.43 us  [correlate(): jnp.einsum('swf,rwf->srf', source_real, panel_imag, preferred_element_typ...]
    dot_general x1, other arithmetic: 2.21 us -> 4.41 us  [correlate(): jnp.einsum('swf,rwf->srf', source_real, panel_real, preferred_element_typ...]
  transfers between devices with their start and end apart: 1 -> 4, of which waited for: 0 -> 1; matrix products, arithmetic and copies ran while one was open for 28% -> 35% of each run, Pallas kernels for 0% -> 0%
where the time goes in v1:
time: 148 us; the launch traced here: 147 us
  other arithmetic  45.7 us (31%)
  local copies, waits for them, and re-layouts  35 us (24%)
  matrix products  25 us (17%)
  blocking collectives  20.5 us (14%)
  between operations  13.7 us (9%)
  starting transfers between devices  4.72 us (3%)
  waiting for transfers between devices  2.5 us (2%)
    another operation x7, other arithmetic  24.8 us
    all_gather x1, blocking collectives, body(): lax.all_gather(mask_rows, 'tile', axis=0, tiled=True)  12 us
    all_gather x1, blocking collectives, body(): lax.all_gather(mask_rows, 'grp', axis=0, tiled=True)  8.49 us
    dot_general x1, matrix products, correlate(): jnp.einsum('swf,rwf->srf', source_imag, panel_imag, preferred_element_typ...  5.49 us
    dot_general x1, matrix products, correlate(): jnp.einsum('swf,rwf->srf', source_real, panel_real, preferred_element_typ...  4.77 us
    dot_general x1, matrix products, correlate(): jnp.einsum('swf,rwf->srf', source_imag, panel_real, preferred_element_typ...  4.76 us
    dot_general x1, matrix products, correlate(): jnp.einsum('swf,rwf->srf', source_real, panel_imag, preferred_element_typ...  4.72 us
    dot_general x1, matrix products, correlate(): jnp.dot(stacked.reshape(-1, 2 * bin_count), lag_basis, preferred_element_...  4.55 us
  transfers between devices with their start and end apart: 4, of which 1 were waited for; matrix products, arithmetic and copies ran while one was open for 35% of the time, Pallas kernels for 0%

profile of v1, /device:TPU:0, one launch (start us, length us, event | category | flops | bytes accessed | tf_op | source)
XLA Modules:
  0.0 147.1 jit_solution(15462794712300790785)
XLA Ops:
  7.5 4.6 %reduce-window.6 = f32[4,16,4,128]{3,1,2,0:T(8,128)S(1)} reduce-window(f32[4,16,4,128]{3,1,2,0:T(8,128)S(1)} %copy_bitcast_fusion.1, f32[]{:T(128)} %constant.113.clone.1), window={size=1x1x1x128 pad=0_0x0_0x0_0x127_0}, to_apply=%region_0.1 | reduce-window | flops 4161536 | bytes 262148 | tf_op jit(solution)/shard_map/reduce-window
  14.6 3.0 %collective-permute-start = (bf16[4,16,1024]{2,1,0:T(8,128)(2,1)S(1)}, bf16[4,16,1024]{2,1,0:T(8,128)(2,1)S(1)}, u32[]{:S(2)}, u32[]{:S(2)}) collective-permute-start(bf16[4,16,1024]{2,1,0:T(8,128)(2,1)S(1)} %pad_maximum_fusion), channel_id=1, source_target_pairs={{0,1},{1,2},{2,3},{3,0},{4,5},{5,6},{6,7},{7,4},{8,9},{9,10},{10,1... | collective-permute-start | bytes 393224 | tf_op jit(solution)/shard_map/ppermute | solution.py:21
  18.7 1.5 %copy.45 = bf16[4,16,1024]{1,0,2:T(4,128)(2,1)S(1)} copy(bf16[4,16,1024]{2,1,0:T(8,128)(2,1)} %copy-done.7) | data formatting | bytes 262144 | tf_op jit(solution)/shard_map/concatenate | solution.py:56
  21.0 8.5 %all-gather = bf16[4,4,16]{2,1,0:T(4,128)(2,1)S(1)} all-gather(bf16[1,4,16]{2,1,0:T(4,128)(2,1)S(1)} %convert_bitcast_fusion), channel_id=1, replica_groups=mesh['tile'=8,'grp'=4] {'grp'}, dimensions={0}, use_global_device_ids=true | all-gather | bytes 640 | tf_op jit(solution)/shard_map/all_gather | solution.py:112
  29.5 12.0 %all-gather.1 = bf16[8,4,16]{2,1,0:T(4,128)(2,1)S(1)} all-gather(bf16[1,4,16]{2,1,0:T(4,128)(2,1)S(1)} %convert_bitcast_fusion), channel_id=1, replica_groups=mesh['tile'=8,'grp'=4] {'tile'}, dimensions={0}, use_global_device_ids=true | all-gather | bytes 1152 | tf_op jit(solution)/shard_map/all_gather | solution.py:105
  42.8 18.2 %cosine_convert_fusion = (bf16[512,2048]{1,0:T(8,128)(2,1)}, bf16[512,2048]{1,0:T(8,128)(2,1)}) fusion(s32[2048]{0:T(1024)S(1)} %iota_add_fusion), kind=kLoop, calls=%fused_computation.13 | loop fusion | flops 17825792 | bytes 4202496 | tf_op jit(solution)/shard_map/convert
  62.4 2.5 %broadcast_in_dim.39 = bf16[16,16,1024]{1,0,2:T(8,128)(2,1)} broadcast(bf16[]{:T(256)} %constant.111.clone.1), dimensions={} | broadcast | bytes 524290 | tf_op jit(solution)/shard_map/broadcast_in_dim | solution.py:16
  71.1 2.5 %collective-permute-done.2 = bf16[4,16,1024]{2,1,0:T(8,128)(2,1)S(1)} collective-permute-done((bf16[4,16,1024]{2,1,0:T(8,128)(2,1)S(1)}, bf16[4,16,1024]{2,1,0:T(8,128)(2,1)S(1)}, u32[]{:S(2)}, u32[]{:S(2)}) %collective-permute-start.2) | collective-permute-done | bytes 131104 | tf_op jit(solution)/shard_map/ppermute | solution.py:21
  75.7 4.4 %fusion.66 = bf16[16,16,1024]{1,0,2:T(8,128)(2,1)} fusion(bf16[16,16,1024]{1,0,2:T(8,128)(2,1)} %constant_dynamic-update-slice_fusion, bf16[16,16]{1,0:T(8,128)(2,1)S(1)} %bitcast.69), kind=kLoop, calls=%fused_computation.18.clone.1 | loop fusion | flops 262144 | bytes 1049088 | tf_op jit(solution)/shard_map/swf,rwf->srf/dot_general | solution.py:77
  80.1 4.4 %fusion.70 = bf16[16,16,1024]{1,0,2:T(8,128)(2,1)} fusion(bf16[16,16,1024]{1,0,2:T(8,128)(2,1)} %constant_dynamic-update-slice_fusion, bf16[16,16]{1,0:T(8,128)(2,1)S(1)} %bitcast.70), kind=kLoop, calls=%fused_computation.22.clone | loop fusion | flops 262144 | bytes 1049088 | tf_op jit(solution)/shard_map/swf,rwf->srf/dot_general | solution.py:78
  84.5 4.4 %fusion.72 = bf16[16,16,1024]{1,0,2:T(8,128)(2,1)} fusion(bf16[16,16,1024]{1,0,2:T(8,128)(2,1)} %constant_dynamic-update-slice_fusion, bf16[16,16]{1,0:T(8,128)(2,1)S(1)} %bitcast.71), kind=kLoop, calls=%fused_computation.24.clone | loop fusion | flops 262144 | bytes 1049088 | tf_op jit(solution)/shard_map/swf,rwf->srf/dot_general | solution.py:80
  89.0 4.4 %fusion.68 = bf16[16,16,1024]{1,0,2:T(8,128)(2,1)} fusion(bf16[16,16,1024]{1,0,2:T(8,128)(2,1)} %constant_dynamic-update-slice_fusion, bf16[16,16]{1,0:T(8,128)(2,1)S(1)} %bitcast.72), kind=kLoop, calls=%fused_computation.20.clone.1 | loop fusion | flops 262144 | bytes 1049088 | tf_op jit(solution)/shard_map/swf,rwf->srf/dot_general | solution.py:75
  93.4 1.8 %gather_fusion = bf16[16,16,1024]{2,1,0:T(8,128)(2,1)S(1)} fusion(bf16[32,16,1024]{2,1,0:T(8,128)(2,1)} %all-gather.4.cloned.1.call-done, s32[1024]{0:T(1024)S(1)} %pad_clamp_fusion), kind=kCustom, calls=%fused_computation | custom fusion | bytes 1048640 | tf_op jit(solution)/shard_map/jit(_take)/gather | solution.py:108
  96.1 2.0 %copy.50 = bf16[16,16,512]{1,0,2:T(8,128)(2,1)S(1)} copy(bf16[16,16,512]{2,1,0:T(8,128)(2,1)S(1)} %get-tuple-element.7) | data formatting | bytes 524288 | tf_op jit(solution)/shard_map/slice | solution.py:72
  98.1 5.5 %fusion.10 = f32[512,16,16]{2,1,0:T(8,128)} fusion(bf16[16,16,512]{1,0,2:T(8,128)(2,1)S(1)} %copy.50, bf16[16,16,1024]{1,0,2:T(8,128)(2,1)} %fusion.66), kind=kOutput, calls=%fused_computation.17 | convolution fusion | flops 4194304 | bytes 1310720 | tf_op jit(solution)/shard_map/swf,rwf->srf/dot_general | solution.py:77
  103.6 3.6 %copy.52 = f32[512,16,16]{0,1,2:T(8,128)} copy(f32[512,16,16]{2,1,0:T(8,128)} %fusion.10) | data formatting | bytes 1048576 | tf_op jit(solution)/shard_map/swf,rwf->srf/dot_general | solution.py:77
  107.2 2.0 %copy.49 = bf16[16,16,512]{1,0,2:T(8,128)(2,1)S(1)} copy(bf16[16,16,512]{2,1,0:T(8,128)(2,1)S(1)} %copy-done.8) | data formatting | bytes 524288 | tf_op jit(solution)/shard_map/slice | solution.py:71
  110.5 4.7 %fusion.14 = f32[512,16,16]{2,1,0:T(8,128)} fusion(bf16[16,16,512]{1,0,2:T(8,128)(2,1)S(1)} %copy.49, bf16[16,16,1024]{1,0,2:T(8,128)(2,1)} %fusion.70), kind=kOutput, calls=%fused_computation.21 | convolution fusion | flops 4194304 | bytes 1310720 | tf_op jit(solution)/shard_map/swf,rwf->srf/dot_general | solution.py:78
  115.2 3.8 %copy.55 = f32[512,16,16]{0,1,2:T(8,128)} copy(f32[512,16,16]{2,1,0:T(8,128)} %fusion.14) | data formatting | bytes 1048576 | tf_op jit(solution)/shard_map/swf,rwf->srf/dot_general | solution.py:78
  119.0 4.8 %fusion.16 = f32[512,16,16]{2,1,0:T(8,128)} fusion(bf16[16,16,512]{1,0,2:T(8,128)(2,1)S(1)} %copy-done.1, bf16[16,16,1024]{1,0,2:T(8,128)(2,1)} %fusion.72), kind=kOutput, calls=%fused_computation.23 | convolution fusion | flops 4194304 | bytes 1310720 | tf_op jit(solution)/shard_map/swf,rwf->srf/dot_general | solution.py:80
  123.8 3.8 %copy.56 = f32[512,16,16]{0,1,2:T(8,128)} copy(f32[512,16,16]{2,1,0:T(8,128)} %fusion.16) | data formatting | bytes 1048576 | tf_op jit(solution)/shard_map/swf,rwf->srf/dot_general | solution.py:80
  127.6 4.8 %fusion.12 = f32[512,16,16]{2,1,0:T(8,128)} fusion(bf16[16,16,512]{1,0,2:T(8,128)(2,1)S(1)} %copy-done.3, bf16[16,16,1024]{1,0,2:T(8,128)(2,1)} %fusion.68), kind=kOutput, calls=%fused_computation.19 | convolution fusion | flops 4194304 | bytes 1310720 | tf_op jit(solution)/shard_map/swf,rwf->srf/dot_general | solution.py:75
  132.4 3.1 %copy.51 = f32[512,16,16]{0,1,2:T(8,128)S(1)} copy(f32[512,16,16]{2,1,0:T(8,128)} %fusion.12) | data formatting | bytes 1048576 | tf_op jit(solution)/shard_map/swf,rwf->srf/dot_general | solution.py:75
  135.7 4.5 %fusion.21 = bf16[256,2048]{1,0:T(8,128)(2,1)} fusion(bf16[512,2048]{1,0:T(8,128)(2,1)} %get-tuple-element.14, bf16[512,2048]{1,0:T(8,128)(2,1)} %get-tuple-element.13, bf16[256,512]{1,0:T(8,128)(2,1)S(1)} %bitcast.66, bf16[256,512]{1,0:T(8,128)(2,1)S(1)} %bitcast.65), kind=kOutput, calls=%fused_computation.26 | convolution fusion | flops 1084227584 | bytes 5767168 | tf_op jit(solution)/shard_map/dot_general | solution.py:84
  (57 shorter events, 18.7 us)
Async XLA Ops:
  6.5 86.8 %all-gather.4.cloned.1.call-start = ((), (), s32[]{:S(2)}) async-start(), calls=%async_computation | async-start | bytes 1179648 | tf_op jit(solution)/shard_map/all_gather | solution.py:104
  14.6 4.1 %copy-start.7 = (bf16[4,16,1024]{2,1,0:T(8,128)(2,1)}, bf16[4,16,1024]{2,1,0:T(8,128)(2,1)S(1)}, u32[]{:S(2)}) copy-start(bf16[4,16,1024]{2,1,0:T(8,128)(2,1)S(1)} %pad_maximum_fusion) | copy-start | bytes 393220
  14.6 51.6 %collective-permute-start = (bf16[4,16,1024]{2,1,0:T(8,128)(2,1)S(1)}, bf16[4,16,1024]{2,1,0:T(8,128)(2,1)S(1)}, u32[]{:S(2)}, u32[]{:S(2)}) collective-permute-start(bf16[4,16,1024]{2,1,0:T(8,128)(2,1)S(1)} %pad_maximum_fusion), channel_id=1, source_target_pairs={{0,1},{1,2},{2,3},{3,0},{4,5},{5,6},{6,7},{7,4},{8,9},{9,10},{10,1... | collective-permute-start | bytes 393224 | tf_op jit(solution)/shard_map/ppermute | solution.py:21
  17.7 51.4 %collective-permute-start.1 = (bf16[4,16,1024]{2,1,0:T(8,128)(2,1)S(1)}, bf16[4,16,1024]{2,1,0:T(8,128)(2,1)S(1)}, u32[]{:S(2)}, u32[]{:S(2)}) collective-permute-start(bf16[4,16,1024]{2,1,0:T(8,128)(2,1)S(1)} %pad_maximum_fusion), channel_id=1, source_target_pairs={{0,3},{1,0},{2,1},{3,2},{4,7},{5,4},{6,5},{7,6},{8,11},{9,8},{10,9... | collective-permute-start | bytes 393224 | tf_op jit(solution)/shard_map/ppermute | solution.py:26
  66.9 6.7 %collective-permute-start.2 = (bf16[4,16,1024]{2,1,0:T(8,128)(2,1)S(1)}, bf16[4,16,1024]{2,1,0:T(8,128)(2,1)S(1)}, u32[]{:S(2)}, u32[]{:S(2)}) collective-permute-start(bf16[4,16,1024]{2,1,0:T(8,128)(2,1)S(1)} %collective-permute-done), channel_id=1, source_target_pairs={{0,1},{1,2},{2,3},{3,0},{4,5},{5,6},{6,7},{7,4},{8,9},{9,10},{10,1... | collective-permute-start | bytes 393224 | tf_op jit(solution)/shard_map/ppermute | solution.py:21
  98.1 5.5 %copy-start = (bf16[16,16,512]{1,0,2:T(8,128)(2,1)}, bf16[16,16,512]{1,0,2:T(8,128)(2,1)S(1)}, u32[]{:S(2)}) copy-start(bf16[16,16,512]{1,0,2:T(8,128)(2,1)S(1)} %copy.50) | copy-start | bytes 786436
  103.6 3.6 %copy-start.8 = (bf16[16,16,512]{2,1,0:T(8,128)(2,1)S(1)}, bf16[16,16,512]{2,1,0:T(8,128)(2,1)}, u32[]{:S(2)}) copy-start(bf16[16,16,512]{2,1,0:T(8,128)(2,1)} %get-tuple-element.8) | copy-start | bytes 786436
  109.2 1.3 copy-start.2
  115.2 3.8 %copy-start.1 = (bf16[16,16,512]{1,0,2:T(8,128)(2,1)S(1)}, bf16[16,16,512]{1,0,2:T(8,128)(2,1)}, u32[]{:S(2)}) copy-start(bf16[16,16,512]{1,0,2:T(8,128)(2,1)} %copy-done) | copy-start | bytes 786436
  123.8 3.8 %copy-start.3 = (bf16[16,16,512]{1,0,2:T(8,128)(2,1)S(1)}, bf16[16,16,512]{1,0,2:T(8,128)(2,1)}, u32[]{:S(2)}) copy-start(bf16[16,16,512]{1,0,2:T(8,128)(2,1)} %copy-done.2) | copy-start | bytes 786436
  132.3 3.1 %copy-start.4 = (f32[512,16,16]{0,1,2:T(8,128)S(1)}, f32[512,16,16]{0,1,2:T(8,128)}, u32[]{:S(2)}) copy-start(f32[512,16,16]{0,1,2:T(8,128)} %copy.52) | copy-start | bytes 1572868
  132.4 3.1 %copy-start.5 = (f32[512,16,16]{0,1,2:T(8,128)S(1)}, f32[512,16,16]{0,1,2:T(8,128)}, u32[]{:S(2)}) copy-start(f32[512,16,16]{0,1,2:T(8,128)} %copy.55) | copy-start | bytes 1572868
  132.4 3.1 %copy-start.6 = (f32[512,16,16]{0,1,2:T(8,128)S(1)}, f32[512,16,16]{0,1,2:T(8,128)}, u32[]{:S(2)}) copy-start(f32[512,16,16]{0,1,2:T(8,128)} %copy.56) | copy-start | bytes 1572868
  132.4 3.1 %copy-start.9 = (f32[16,16]{1,0:T(8,128)S(1)}, f32[16,16]{1,0:T(8,128)}, u32[]{:S(2)}) copy-start(f32[16,16]{1,0:T(8,128)} %fusion.28) | copy-start | bytes 3076
Sparse Core Ops, SparseCore 0:
  18.8 22.9 all-gather.3
